TPU v7x, 32 devices: a whole 2x2x4 slice. The times are simulated.
32 devices in a mesh: groups: 2 (over x), tensor: 16 (over z, y, core).
Axes of the slice: x: 2, y: 2, z: 4, core: 2. Of those that a mesh axis runs over, the one named last changes fastest.
Arguments:
- image_features: bfloat16 [256, 12800], P('groups', 'tensor'), parts along dimension 0, may hold values from -6 to 6
- image_counts: int32 [4], P('groups'), parts along dimension 0, may hold values from 1 to 64, 80 in all
- slot_position: int32 [256], P('groups'), parts along dimension 0, may hold values from 0 to 255, as said below
- text_ids: int32 [512], P('groups'), parts along dimension 0, may hold values from 0 to 49151
- norm_gain: float32 [12800], replicated, may hold values from 0.5 to 1.5
- norm_bias: float32 [12800], replicated, may hold values from -3 to 3
- proj_first: bfloat16 [6144, 12800], P('tensor'), may hold values from -0.0546875 to 0.0546875
- proj_second: bfloat16 [6144, 6144], P('tensor'), may hold values from -0.078125 to 0.078125
- embedding: bfloat16 [6144, 49152], P('tensor'), may hold values from -6 to 6
- rms_gain: float32 [6144], replicated, may hold values from 0.5 to 1.5
- gate_weight: bfloat16 [6144, 16384], P(None, 'tensor'), may hold values from -0.109375 to 0.109375
- up_weight: bfloat16 [6144, 16384], P(None, 'tensor'), may hold values from -0.109375 to 0.109375
- down_weight: bfloat16 [16384, 6144], P('tensor'), may hold values from -0.046875 to 0.046875
- output_grad: bfloat16 [512, 6144], P('groups', 'tensor'), parts along dimension 0, may hold values from -6 to 6
Outputs:
- input_grad: float32 [512, 6144], P('groups', 'tensor'), parts along dimension 0
- second_grad: float32 [12288, 6144], P(('groups', 'tensor')), parts along dimension 0
There are 2 independent parts, one for each index of `groups`. A program takes and returns all parts, laid end to end along the dimension named above; an argument that names none is the same for every part. Nothing has to cross between parts.
Inputs may be any that keep to these rules, and one draw needn't show every extreme that they name: `image_counts`: the counts sum to 80. `slot_position`: the 128 positions are distinct.
All inputs are finite; a program needn't handle non-finite values.
Results may differ from a plain program's by a relative error of at most 0.0079.
Values may be sent and summed in bfloat16 or wider, within the bound.
No kernel may reach another device: no remote copies, remote signals or barrier semaphores. Data moves between devices by JAX's collectives and lax.ppermute only.
A program may use at most 192 MiB of HBM per device.

v0:
```python
import jax
import jax.numpy as jnp
from jax import lax
from jax.sharding import PartitionSpec as P

LIVE = 80


def layer_norm(rows_in, gain_in, bias_in):
    values = rows_in.astype(jnp.float32)
    centre = values - jnp.mean(values, axis=-1, keepdims=True)
    spread = jnp.mean(centre * centre, axis=-1, keepdims=True)
    return (centre * lax.rsqrt(spread + 1e-05) * gain_in + bias_in).astype(jnp.bfloat16)


def on_device(
    image_features,
    image_counts,
    slot_position,
    text_ids,
    norm_gain,
    norm_bias,
    proj_first,
    proj_second,
    embedding,
    rms_gain,
    gate_weight,
    up_weight,
    down_weight,
    output_grad,
):
    slot_total = image_features.shape[0]
    per_image = slot_total // image_counts.shape[0]
    seq_len = output_grad.shape[0]
    model_width = gate_weight.shape[0]
    col_count = output_grad.shape[1]
    slot_ids = jnp.arange(slot_total, dtype=jnp.int32)
    is_live = slot_ids % per_image < jnp.repeat(
        image_counts, per_image, total_repeat_length=slot_total
    )
    packed_order = jnp.argsort(jnp.where(is_live, 0, 1).astype(jnp.int32), stable=True)[:LIVE]
    gathered = lax.all_gather(image_features[packed_order], "tensor", axis=1, tiled=True)
    positions = slot_position[packed_order]
    in_use = jnp.ones((LIVE,), dtype=bool)
    normed = layer_norm(gathered, norm_gain, norm_bias)
    hidden_pre = lax.dot_general(
        normed, proj_first, (((1,), (1,)), ((), ())), preferred_element_type=jnp.float32
    )
    act_cols = jax.nn.gelu(hidden_pre, approximate=False).astype(jnp.bfloat16)
    act_full = lax.all_gather(act_cols, "tensor", axis=1, tiled=True)
    projected = lax.dot_general(
        act_full, proj_second, (((1,), (1,)), ((), ())), preferred_element_type=jnp.float32
    ).astype(jnp.bfloat16)
    target = jnp.where(in_use, positions, seq_len)
    text_rows = jnp.take(embedding, text_ids, axis=1).T
    tokens = text_rows.at[target].set(projected, mode="drop")
    full_tokens = lax.all_gather(tokens, "tensor", axis=1, tiled=True)
    values = full_tokens.astype(jnp.float32)
    inverse = lax.rsqrt(jnp.mean(values * values, axis=-1, keepdims=True) + 1e-05)
    normed_tokens = (values * inverse * rms_gain).astype(jnp.bfloat16)
    gate_out = jnp.dot(normed_tokens, gate_weight, preferred_element_type=jnp.float32)
    up_out = jnp.dot(normed_tokens, up_weight, preferred_element_type=jnp.float32)
    hidden_grad = lax.dot_general(
        lax.all_gather(output_grad, "tensor", axis=1, tiled=True),
        down_weight,
        (((1,), (1,)), ((), ())),
        preferred_element_type=jnp.float32,
    )
    sig_gate = jax.nn.sigmoid(gate_out)
    gate_grad = (hidden_grad * up_out * sig_gate * (1.0 + gate_out * (1.0 - sig_gate))).astype(
        jnp.bfloat16
    )
    up_grad = (hidden_grad * gate_out * sig_gate).astype(jnp.bfloat16)
    partial_value = lax.dot_general(
        gate_grad, gate_weight, (((1,), (1,)), ((), ())), preferred_element_type=jnp.float32
    )
    partial_value = partial_value + lax.dot_general(
        up_grad, up_weight, (((1,), (1,)), ((), ())), preferred_element_type=jnp.float32
    )
    norm_grad = lax.psum_scatter(partial_value, "tensor", scatter_dimension=1, tiled=True)
    offset = lax.axis_index("tensor") * col_count
    gain_cols = lax.dynamic_slice_in_dim(rms_gain, offset, col_count, 0)
    unit_cols = tokens.astype(jnp.float32) * inverse
    scaled = gain_cols * norm_grad
    row_sums = lax.psum(jnp.sum(scaled * unit_cols, axis=-1), "tensor")
    input_grad = output_grad.astype(jnp.float32) + inverse * (
        scaled - unit_cols * (row_sums / model_width)[:, None]
    )
    proj_grad = jnp.where(in_use[:, None], input_grad[positions], 0.0).astype(jnp.bfloat16)
    second_grad = lax.dot_general(
        proj_grad, act_full, (((0,), (0,)), ((), ())), preferred_element_type=jnp.float32
    )
    return (input_grad, second_grad)


def solution(mesh):
    placed = (
        P("groups", "tensor"),
        P("groups"),
        P("groups"),
        P("groups"),
        P(),
        P(),
        P("tensor", None),
        P("tensor", None),
        P("tensor", None),
        P(),
        P(None, "tensor"),
        P(None, "tensor"),
        P("tensor", None),
        P("groups", "tensor"),
    )
    return jax.shard_map(
        on_device,
        mesh=mesh,
        in_specs=placed,
        out_specs=(P("groups", "tensor"), P(("groups", "tensor"), None)),
        check_vma=False,
    )
```

profile of v0, /device:TPU:0, one launch (start us, length us, event | category | flops | bytes accessed | tf_op | source)
XLA Modules:
  0.0 335.2 jit_solution(3321569869737275003)
XLA Ops:
  7.2 1.3 fusion.38
  8.5 2.0 compare_select_fusion.3
  10.5 2.5 sort.17
  14.1 1.4 gather_fusion.2
  16.4 46.7 %copy.21 = bf16[384,49152]{0,1:T(8,128)(2,1)} copy(bf16[384,49152]{1,0:T(8,128)(2,1)} %param.24) | data formatting | bytes 75497472 | tf_op args[8]
  63.1 1.2 gather_fusion.1
  64.3 2.8 gather_fusion
  67.3 4.4 %copy.23 = f32[16,800,80]{1,0,2:T(8,128)} copy(bf16[16,800,80]{1,2,0:T(8,128)(2,1)} %all-gather.10.cloned.1.call-done) | data formatting | bytes 6144000 | tf_op jit(solution)/shard_map/convert_element_type | solution.py:10
  71.7 5.9 %reshape.138 = f32[12800,80]{0,1:T(8,128)} reshape(f32[16,800,80]{1,0,2:T(8,128)} %copy.23) | data formatting | bytes 8192000 | tf_op jit(solution)/shard_map/convert_element_type | solution.py:10
  78.0 2.9 multiply_reduce_fusion
  81.0 7.5 %fusion.23 = bf16[80,384]{1,0:T(8,128)(2,1)S(1)} fusion(bf16[384,12800]{1,0:T(8,128)(2,1)} %param.22, f32[12800,80]{0,1:T(8,128)S(1)} %copy-done.2, f32[12800]{0:T(1024)S(1)} %copy-done.10, f32[80]{0:T(128)S(1)} %add_rsqrt_fusion.1, f32[80]{0:T(128)S(1)} %broadcast_multiply_fusion.1, f32[12800]{0:T(1024)S(1)} %copy-done.11), kind=kOutput, calls=%fused_computation.38 | convolution fusion | flops 793548800 | bytes 14090880 | tf_op jit(solution)/shard_map/dot_general | solution.py:46
  88.5 29.3 %all_gather.13 = bf16[80,6144]{1,0:T(8,128)(2,1)S(1)} all-gather(bf16[80,384]{1,0:T(8,128)(2,1)S(1)} %fusion.23), channel_id=1, replica_groups=mesh['groups'=2,'tensor'=16] {'tensor'}, dimensions={1}, use_global_device_ids=true | all-gather | bytes 1044480 | tf_op jit(solution)/shard_map/all_gather | solution.py:50
  117.8 1.5 convolution_convert_fusion
  121.3 7.5 %fusion.39 = f32[256,1024]{1,0:T(8,128)S(1)} fusion(bf16[256,6144]{1,0:T(8,128)(2,1)} %all-gather.8.cloned.1.call-done, bf16[1024,6144]{1,0:T(8,128)(2,1)} %param.28), kind=kOutput, calls=%fused_computation.73 | convolution fusion | flops 3221225472 | bytes 16777216 | tf_op jit(solution)/shard_map/dot_general | solution.py:63
  128.8 35.8 %all-gather.6.cloned.1.call-done = bf16[256,6144]{1,0:T(8,128)(2,1)} async-done(((bf16[256,384]{1,0:T(8,128)(2,1)}), bf16[256,6144]{1,0:T(8,128)(2,1)}) %all-gather.6.cloned.1.call-update) | async-done | bytes 3145744 | tf_op jit(solution)/shard_map/all_gather | solution.py:57
  164.7 2.6 fusion
  167.3 10.0 %fusion.13 = f32[256,1024]{1,0:T(8,128)} fusion(bf16[6144,1024]{1,0:T(8,128)(2,1)} %param.26, bf16[256,6144]{1,0:T(8,128)(2,1)} %all-gather.6.cloned.1.call-done, f32[6144]{0:T(1024)S(1)} %copy-done.9, f32[256]{0:T(256)S(1)} %add_rsqrt_fusion), kind=kOutput, calls=%fused_computation.27 | convolution fusion | flops 3227516928 | bytes 16802816 | tf_op jit(solution)/shard_map/dot_general | solution.py:61
  177.3 16.0 %fusion.17 = f32[256,6144]{1,0:T(8,128)} fusion(bf16[6144,1024]{1,0:T(8,128)(2,1)} %param.26, f32[256,1024]{1,0:T(8,128)S(1)} %fusion.39, bf16[6144,1024]{1,0:T(8,128)(2,1)} %param.27, f32[256,1024]{1,0:T(8,128)} %fusion.13, bf16[256,6144]{1,0:T(8,128)(2,1)} %all-gather.6.cloned.1.call-done, f32[6144]{0:T(1024)S(1)} %copy-done.9, f32[256]{0:T(256)S(1)} %add_rsqrt_fusion), kind=kOutput, calls=%fused_computation.28 | convolution fusion | flops 6451363840 | bytes 36725760 | tf_op jit(solution)/shard_map/dot_general | solution.py:74
  193.3 12.9 %convolution_add_fusion = f32[256,6144]{1,0:T(8,128)} fusion(f32[256,6144]{1,0:T(8,128)} %fusion.17, bf16[6144,1024]{1,0:T(8,128)(2,1)} %param.27, f32[256,1024]{1,0:T(8,128)S(1)} %fusion.39, f32[256,1024]{1,0:T(8,128)} %fusion.13), kind=kOutput, calls=%fused_computation.7 | convolution fusion | flops 3224371200 | bytes 27262976 | tf_op jit(solution)/shard_map/dot_general | solution.py:77
  206.3 83.2 %reduce-scatter.2.cloned.1.call-done = f32[256,384]{1,0:T(8,128)} async-done(((f32[256,6144]{1,0:T(8,128)}), f32[256,384]{1,0:T(8,128)}) %reduce-scatter.2.cloned.1.call-update) | async-done | bytes 393232 | tf_op jit(solution)/shard_map/reduce_scatter | solution.py:80
  289.5 1.2 multiply_reduce_fusion.1
  290.7 30.8 %psum.7 = f32[256]{0:T(256)S(1)} all-reduce(f32[256]{0:T(256)S(1)} %multiply_reduce_fusion.1), channel_id=1, replica_groups=mesh['groups'=2,'tensor'=16] {'tensor'}, use_global_device_ids=true, to_apply=%region_7.8 | all-reduce | flops 256 | bytes 2048 | tf_op jit(solution)/shard_map/psum | solution.py:85
  321.6 1.2 multiply_add_fusion
  323.5 5.2 %fusion.40 = f32[384,6144]{1,0:T(8,128)} fusion(bf16[80,384]{1,0:T(8,128)(2,1)S(1)} %gather_fusion.3, bf16[80,6144]{1,0:T(8,128)(2,1)S(1)} %all_gather.13), kind=kOutput, calls=%fused_computation.74 | convolution fusion | flops 377487360 | bytes 10481664 | tf_op jit(solution)/shard_map/dot_general | solution.py:90
  (57 shorter events, 5.3 us)
Async XLA Ops:
  7.2 55.9 %copy-start = (s32[128]{0:T(128)S(1)}, s32[128]{0:T(128)}, u32[]{:S(2)}) copy-start(s32[128]{0:T(128)} %param.18) | copy-start | bytes 1540
  7.2 60.1 %all-gather.10.cloned.1.call-start = ((), (), s32[]{:S(2)}) async-start(), calls=%async_computation.4 | async-start | bytes 2437120 | tf_op jit(solution)/shard_map/all_gather | solution.py:42
  15.6 105.8 %all-gather.8.cloned.1.call-start = ((), (), s32[]{:S(2)}) async-start(), calls=%async_computation.2 | async-start | bytes 3342336 | tf_op jit(solution)/shard_map/all_gather | solution.py:64
  16.3 48.0 %copy-start.8 = (s32[256]{0:T(256)S(1)}, s32[256]{0:T(256)}, u32[]{:S(2)}) copy-start(s32[256]{0:T(256)} %param.19) | copy-start | bytes 3076
  16.3 148.3 %all-gather.6.cloned.1.call-start = ((), (), s32[]{:S(2)}) async-start(), calls=%async_computation.1 | async-start | bytes 3342336 | tf_op jit(solution)/shard_map/all_gather | solution.py:57
  67.3 10.3 %copy-start.3 = (bf16[16,800,80]{1,2,0:T(8,128)(2,1)S(1)}, bf16[16,800,80]{1,2,0:T(8,128)(2,1)}, u32[]{:S(2)}) copy-start(bf16[16,800,80]{1,2,0:T(8,128)(2,1)} %all-gather.10.cloned.1.call-done) | copy-start | bytes 6144004
  71.7 9.3 %copy-start.10 = (f32[12800]{0:T(1024)S(1)}, f32[12800]{0:T(1024)}, u32[]{:S(2)}) copy-start(f32[12800]{0:T(1024)} %param.20) | copy-start | bytes 153604
  71.7 9.3 %copy-start.11 = (f32[12800]{0:T(1024)S(1)}, f32[12800]{0:T(1024)}, u32[]{:S(2)}) copy-start(f32[12800]{0:T(1024)} %param.21) | copy-start | bytes 153604
  77.6 3.4 %copy-start.2 = (f32[12800,80]{0,1:T(8,128)S(1)}, f32[12800,80]{0,1:T(8,128)}, u32[]{:S(2)}) copy-start(f32[12800,80]{0,1:T(8,128)} %reshape.138) | copy-start | bytes 12288004
  78.0 39.8 %slice-start = ((s8[4718592]{0:T(1024)(128)(4,1)}), s8[4194304]{0:T(1024)(128)(4,1)S(1)}, s32[]{:S(2)}) async-start(s8[4718592]{0:T(1024)(128)(4,1)} %bitcast.29), calls=%async_computation.5 | async-start | bytes 8388608
  81.0 36.8 %slice-start.1 = ((s8[4718592]{0:T(1024)(128)(4,1)}), s8[524288]{0:T(1024)(128)(4,1)S(1)}, s32[]{:S(2)}) async-start(s8[4718592]{0:T(1024)(128)(4,1)} %bitcast.29), calls=%async_computation.6 | async-start | bytes 1048576
  120.4 0.7 copy-start.4
  121.1 46.2 %copy-start.9 = (f32[6144]{0:T(1024)S(1)}, f32[6144]{0:T(1024)}, u32[]{:S(2)}) copy-start(f32[6144]{0:T(1024)} %param.25) | copy-start | bytes 73732
  121.1 168.5 %reduce-scatter.2.cloned.1.call-start = ((), (), s32[]{:S(2)}) async-start(), calls=%async_computation.3 | async-start | bytes 6684672 | tf_op jit(solution)/shard_map/reduce_scatter | solution.py:80
  206.2 83.4 %copy-start.5 = (bf16[256,384]{1,0:T(8,128)(2,1)S(1)}, bf16[256,384]{1,0:T(8,128)(2,1)}, u32[]{:S(2)}) copy-start(bf16[256,384]{1,0:T(8,128)(2,1)} %copy-done.4) | copy-start | bytes 589828
  206.2 115.4 %copy-start.7 = (bf16[256,384]{1,0:T(8,128)(2,1)S(1)}, bf16[256,384]{1,0:T(8,128)(2,1)}, u32[]{:S(2)}) copy-start(bf16[256,384]{1,0:T(8,128)(2,1)} %param.29) | copy-start | bytes 589828
  206.3 122.3 %copy-start.1 = (s32[128]{0:T(128)S(1)}, s32[128]{0:T(128)}, u32[]{:S(2)}) copy-start(s32[128]{0:T(128)} %param.18) | copy-start | bytes 1540
  322.8 5.9 %copy-start.6 = (f32[256,384]{1,0:T(8,128)}, f32[256,384]{1,0:T(8,128)S(1)}, u32[]{:S(2)}) copy-start(f32[256,384]{1,0:T(8,128)S(1)} %multiply_add_fusion) | copy-start | bytes 1179652
Sparse Core Ops, SparseCore 0:
  15.7 45.1 all-gather.9
  63.0 48.9 all-gather.7
  121.2 43.4 all-gather.5
  206.3 83.1 reduce-scatter.1
where the time goes:
time: 337 us; the launch traced here: 335 us
  waiting for transfers between devices  120 us (36%)
  local copies, waits for them, and re-layouts  67.3 us (20%)
  matrix products  60.5 us (18%)
  blocking collectives  60.1 us (18%)
  between operations  14 us (4%)
  other arithmetic  13 us (4%)
    reduce_scatter x1, waiting for transfers between devices, on_device(): lax.psum_scatter(partial_value, 'tensor', scatter_dimension=1, tiled=True)  83.2 us
    unnamed x30, local copies, waits for them, and re-layouts  48.5 us
    all_gather x1, waiting for transfers between devices, on_device(): full_tokens = lax.all_gather(tokens, 'tensor', axis=1, tiled=True)  35.8 us
    psum x1, blocking collectives, on_device(): row_sums = lax.psum(jnp.sum(scaled * unit_cols, axis=-1), 'tensor')  30.8 us
    all_gather x1, blocking collectives, on_device(): act_full = lax.all_gather(act_cols, 'tensor', axis=1, tiled=True)  29.3 us
    dot_general x1, matrix products, on_device(): lax.dot_general(gate_grad, gate_weight, (((1,), (1,)), ((), ())), preferr...  16 us
    dot_general x1, matrix products, on_device(): lax.dot_general(up_grad, up_weight, (((1,), (1,)), ((), ())), preferred_e...  12.9 us
    convert_element_type x2, local copies, waits for them, and re-layouts, layer_norm(): values = rows_in.astype(jnp.float32)  10.3 us
  transfers between devices with their start and end apart: 4, of which 2 were waited for; matrix products, arithmetic and copies ran while one was open for 24% of the time, Pallas kernels for 0%

commit v1 on v0

--- a/solution.py
+++ b/solution.py
@@ -82,7 +82,7 @@
     gain_cols = lax.dynamic_slice_in_dim(rms_gain, offset, col_count, 0)
     unit_cols = tokens.astype(jnp.float32) * inverse
     scaled = gain_cols * norm_grad
-    row_sums = lax.psum(jnp.sum(scaled * unit_cols, axis=-1), "tensor")
+    row_sums = jnp.sum(lax.all_gather(jnp.sum(scaled * unit_cols, axis=-1), "tensor"), axis=0)
     input_grad = output_grad.astype(jnp.float32) + inverse * (
         scaled - unit_cols * (row_sums / model_width)[:, None]
     )

time: 337 us -> 326 us (0.967)
  blocking collectives: 60.1 us -> 48.9 us
    psum x1 -> x0, blocking collectives: 30.8 us -> none  [on_device(): row_sums = lax.psum(jnp.sum(scaled * unit_cols, axis=-1), 'tensor')]
    all_gather x0 -> x1, blocking collectives: none -> 19.6 us  [on_device(): lax.all_gather(jnp.sum(scaled * unit_cols, axis=-1), 'tensor')]
  transfers between devices with their start and end apart: 4 -> 4, of which waited for: 2 -> 2; matrix products, arithmetic and copies ran while one was open for 24% -> 25% of each run, Pallas kernels for 0% -> 0%
where the time goes in v1:
time: 326 us; the launch traced here: 324 us
  waiting for transfers between devices  120 us (37%)
  local copies, waits for them, and re-layouts  67.3 us (21%)
  matrix products  60.5 us (19%)
  blocking collectives  48.9 us (15%)
  between operations  14 us (4%)
  other arithmetic  13 us (4%)
    reduce_scatter x1, waiting for transfers between devices, on_device(): lax.psum_scatter(partial_value, 'tensor', scatter_dimension=1, tiled=True)  83.2 us
    unnamed x30, local copies, waits for them, and re-layouts  48.5 us
    all_gather x1, waiting for transfers between devices, on_device(): full_tokens = lax.all_gather(tokens, 'tensor', axis=1, tiled=True)  35.8 us
    all_gather x1, blocking collectives, on_device(): act_full = lax.all_gather(act_cols, 'tensor', axis=1, tiled=True)  29.3 us
    all_gather x1, blocking collectives, on_device(): lax.all_gather(jnp.sum(scaled * unit_cols, axis=-1), 'tensor')  19.6 us
    dot_general x1, matrix products, on_device(): lax.dot_general(gate_grad, gate_weight, (((1,), (1,)), ((), ())), preferr...  16 us
    dot_general x1, matrix products, on_device(): lax.dot_general(up_grad, up_weight, (((1,), (1,)), ((), ())), preferred_e...  12.9 us
    convert_element_type x2, local copies, waits for them, and re-layouts, layer_norm(): values = rows_in.astype(jnp.float32)  10.3 us
  transfers between devices with their start and end apart: 4, of which 2 were waited for; matrix products, arithmetic and copies ran while one was open for 25% of the time, Pallas kernels for 0%

profile of v1, /device:TPU:0, one launch (start us, length us, event | category | flops | bytes accessed | tf_op | source)
XLA Modules:
  0.0 324.0 jit_solution(12364418901481566084)
XLA Ops:
  7.2 1.3 fusion.38
  8.5 2.0 compare_select_fusion.3
  10.5 2.5 sort.17
  14.1 1.4 gather_fusion.2
  16.4 46.7 %copy.21 = bf16[384,49152]{0,1:T(8,128)(2,1)} copy(bf16[384,49152]{1,0:T(8,128)(2,1)} %param.24) | data formatting | bytes 75497472 | tf_op args[8]
  63.1 1.2 gather_fusion.1
  64.3 2.8 gather_fusion
  67.3 4.4 %copy.23 = f32[16,800,80]{1,0,2:T(8,128)} copy(bf16[16,800,80]{1,2,0:T(8,128)(2,1)} %all-gather.12.cloned.1.call-done) | data formatting | bytes 6144000 | tf_op jit(solution)/shard_map/convert_element_type | solution.py:10
  71.7 5.9 %reshape.144 = f32[12800,80]{0,1:T(8,128)} reshape(f32[16,800,80]{1,0,2:T(8,128)} %copy.23) | data formatting | bytes 8192000 | tf_op jit(solution)/shard_map/convert_element_type | solution.py:10
  78.0 2.9 multiply_reduce_fusion
  81.0 7.5 %fusion.23 = bf16[80,384]{1,0:T(8,128)(2,1)S(1)} fusion(bf16[384,12800]{1,0:T(8,128)(2,1)} %param.22, f32[12800,80]{0,1:T(8,128)S(1)} %copy-done.2, f32[12800]{0:T(1024)S(1)} %copy-done.10, f32[80]{0:T(128)S(1)} %add_rsqrt_fusion.1, f32[80]{0:T(128)S(1)} %broadcast_multiply_fusion.1, f32[12800]{0:T(1024)S(1)} %copy-done.11), kind=kOutput, calls=%fused_computation.38 | convolution fusion | flops 793548800 | bytes 14090880 | tf_op jit(solution)/shard_map/dot_general | solution.py:46
  88.5 29.3 %all_gather.19 = bf16[80,6144]{1,0:T(8,128)(2,1)S(1)} all-gather(bf16[80,384]{1,0:T(8,128)(2,1)S(1)} %fusion.23), channel_id=1, replica_groups=mesh['groups'=2,'tensor'=16] {'tensor'}, dimensions={1}, use_global_device_ids=true | all-gather | bytes 1044480 | tf_op jit(solution)/shard_map/all_gather | solution.py:50
  117.8 1.5 convolution_convert_fusion
  121.3 7.5 %fusion.39 = f32[256,1024]{1,0:T(8,128)S(1)} fusion(bf16[256,6144]{1,0:T(8,128)(2,1)} %all-gather.10.cloned.1.call-done, bf16[1024,6144]{1,0:T(8,128)(2,1)} %param.28), kind=kOutput, calls=%fused_computation.73 | convolution fusion | flops 3221225472 | bytes 16777216 | tf_op jit(solution)/shard_map/dot_general | solution.py:63
  128.8 35.8 %all-gather.8.cloned.1.call-done = bf16[256,6144]{1,0:T(8,128)(2,1)} async-done(((bf16[256,384]{1,0:T(8,128)(2,1)}), bf16[256,6144]{1,0:T(8,128)(2,1)}) %all-gather.8.cloned.1.call-update) | async-done | bytes 3145744 | tf_op jit(solution)/shard_map/all_gather | solution.py:57
  164.7 2.6 fusion
  167.3 10.0 %fusion.13 = f32[256,1024]{1,0:T(8,128)} fusion(bf16[6144,1024]{1,0:T(8,128)(2,1)} %param.26, bf16[256,6144]{1,0:T(8,128)(2,1)} %all-gather.8.cloned.1.call-done, f32[6144]{0:T(1024)S(1)} %copy-done.9, f32[256]{0:T(256)S(1)} %add_rsqrt_fusion), kind=kOutput, calls=%fused_computation.27 | convolution fusion | flops 3227516928 | bytes 16802816 | tf_op jit(solution)/shard_map/dot_general | solution.py:61
  177.3 16.0 %fusion.17 = f32[256,6144]{1,0:T(8,128)} fusion(bf16[6144,1024]{1,0:T(8,128)(2,1)} %param.26, f32[256,1024]{1,0:T(8,128)S(1)} %fusion.39, bf16[6144,1024]{1,0:T(8,128)(2,1)} %param.27, f32[256,1024]{1,0:T(8,128)} %fusion.13, bf16[256,6144]{1,0:T(8,128)(2,1)} %all-gather.8.cloned.1.call-done, f32[6144]{0:T(1024)S(1)} %copy-done.9, f32[256]{0:T(256)S(1)} %add_rsqrt_fusion), kind=kOutput, calls=%fused_computation.28 | convolution fusion | flops 6451363840 | bytes 36725760 | tf_op jit(solution)/shard_map/dot_general | solution.py:74
  193.3 12.9 %convolution_add_fusion = f32[256,6144]{1,0:T(8,128)} fusion(f32[256,6144]{1,0:T(8,128)} %fusion.17, bf16[6144,1024]{1,0:T(8,128)(2,1)} %param.27, f32[256,1024]{1,0:T(8,128)S(1)} %fusion.39, f32[256,1024]{1,0:T(8,128)} %fusion.13), kind=kOutput, calls=%fused_computation.7 | convolution fusion | flops 3224371200 | bytes 27262976 | tf_op jit(solution)/shard_map/dot_general | solution.py:77
  206.3 83.2 %reduce-scatter.2.cloned.1.call-done = f32[256,384]{1,0:T(8,128)} async-done(((f32[256,6144]{1,0:T(8,128)}), f32[256,384]{1,0:T(8,128)}) %reduce-scatter.2.cloned.1.call-update) | async-done | bytes 393232 | tf_op jit(solution)/shard_map/reduce_scatter | solution.py:80
  289.5 1.2 multiply_reduce_fusion.1
  290.7 19.6 %all-gather.3 = f32[16,1,256]{2,1,0:T(1,128)S(1)} all-gather(f32[1,1,256]{2,1,0:T(1,128)S(1)} %bitcast.33), channel_id=3, replica_groups=mesh['groups'=2,'tensor'=16] {'tensor'}, dimensions={0}, use_global_device_ids=true | all-gather | bytes 17408 | tf_op jit(solution)/shard_map/all_gather | solution.py:85
  310.4 1.2 multiply_add_fusion
  312.3 5.2 %fusion.40 = f32[384,6144]{1,0:T(8,128)} fusion(bf16[80,384]{1,0:T(8,128)(2,1)S(1)} %gather_fusion.3, bf16[80,6144]{1,0:T(8,128)(2,1)S(1)} %all_gather.19), kind=kOutput, calls=%fused_computation.74 | convolution fusion | flops 377487360 | bytes 10481664 | tf_op jit(solution)/shard_map/dot_general | solution.py:90
  (58 shorter events, 5.4 us)
Async XLA Ops:
  7.2 55.9 %copy-start = (s32[128]{0:T(128)S(1)}, s32[128]{0:T(128)}, u32[]{:S(2)}) copy-start(s32[128]{0:T(128)} %param.18) | copy-start | bytes 1540
  7.2 60.1 %all-gather.12.cloned.1.call-start = ((), (), s32[]{:S(2)}) async-start(), calls=%async_computation.4 | async-start | bytes 2437120 | tf_op jit(solution)/shard_map/all_gather | solution.py:42
  15.6 105.8 %all-gather.10.cloned.1.call-start = ((), (), s32[]{:S(2)}) async-start(), calls=%async_computation.2 | async-start | bytes 3342336 | tf_op jit(solution)/shard_map/all_gather | solution.py:64
  16.3 48.0 %copy-start.8 = (s32[256]{0:T(256)S(1)}, s32[256]{0:T(256)}, u32[]{:S(2)}) copy-start(s32[256]{0:T(256)} %param.19) | copy-start | bytes 3076
  16.3 148.3 %all-gather.8.cloned.1.call-start = ((), (), s32[]{:S(2)}) async-start(), calls=%async_computation.1 | async-start | bytes 3342336 | tf_op jit(solution)/shard_map/all_gather | solution.py:57
  67.3 10.3 %copy-start.3 = (bf16[16,800,80]{1,2,0:T(8,128)(2,1)S(1)}, bf16[16,800,80]{1,2,0:T(8,128)(2,1)}, u32[]{:S(2)}) copy-start(bf16[16,800,80]{1,2,0:T(8,128)(2,1)} %all-gather.12.cloned.1.call-done) | copy-start | bytes 6144004
  71.7 9.3 %copy-start.10 = (f32[12800]{0:T(1024)S(1)}, f32[12800]{0:T(1024)}, u32[]{:S(2)}) copy-start(f32[12800]{0:T(1024)} %param.20) | copy-start | bytes 153604
  71.7 9.3 %copy-start.11 = (f32[12800]{0:T(1024)S(1)}, f32[12800]{0:T(1024)}, u32[]{:S(2)}) copy-start(f32[12800]{0:T(1024)} %param.21) | copy-start | bytes 153604
  77.6 3.4 %copy-start.2 = (f32[12800,80]{0,1:T(8,128)S(1)}, f32[12800,80]{0,1:T(8,128)}, u32[]{:S(2)}) copy-start(f32[12800,80]{0,1:T(8,128)} %reshape.144) | copy-start | bytes 12288004
  78.0 39.8 %slice-start = ((s8[4718592]{0:T(1024)(128)(4,1)}), s8[4194304]{0:T(1024)(128)(4,1)S(1)}, s32[]{:S(2)}) async-start(s8[4718592]{0:T(1024)(128)(4,1)} %bitcast.30), calls=%async_computation.5 | async-start | bytes 8388608
  81.0 36.8 %slice-start.1 = ((s8[4718592]{0:T(1024)(128)(4,1)}), s8[524288]{0:T(1024)(128)(4,1)S(1)}, s32[]{:S(2)}) async-start(s8[4718592]{0:T(1024)(128)(4,1)} %bitcast.30), calls=%async_computation.6 | async-start | bytes 1048576
  120.4 0.7 copy-start.4
  121.1 46.2 %copy-start.9 = (f32[6144]{0:T(1024)S(1)}, f32[6144]{0:T(1024)}, u32[]{:S(2)}) copy-start(f32[6144]{0:T(1024)} %param.25) | copy-start | bytes 73732
  121.1 168.5 %reduce-scatter.2.cloned.1.call-start = ((), (), s32[]{:S(2)}) async-start(), calls=%async_computation.3 | async-start | bytes 6684672 | tf_op jit(solution)/shard_map/reduce_scatter | solution.py:80
  206.2 83.4 %copy-start.5 = (bf16[256,384]{1,0:T(8,128)(2,1)S(1)}, bf16[256,384]{1,0:T(8,128)(2,1)}, u32[]{:S(2)}) copy-start(bf16[256,384]{1,0:T(8,128)(2,1)} %copy-done.4) | copy-start | bytes 589828
  206.2 104.2 %copy-start.7 = (bf16[256,384]{1,0:T(8,128)(2,1)S(1)}, bf16[256,384]{1,0:T(8,128)(2,1)}, u32[]{:S(2)}) copy-start(bf16[256,384]{1,0:T(8,128)(2,1)} %param.29) | copy-start | bytes 589828
  206.3 111.2 %copy-start.1 = (s32[128]{0:T(128)S(1)}, s32[128]{0:T(128)}, u32[]{:S(2)}) copy-start(s32[128]{0:T(128)} %param.18) | copy-start | bytes 1540
  311.6 5.9 %copy-start.6 = (f32[256,384]{1,0:T(8,128)}, f32[256,384]{1,0:T(8,128)S(1)}, u32[]{:S(2)}) copy-start(f32[256,384]{1,0:T(8,128)S(1)} %multiply_add_fusion) | copy-start | bytes 1179652
Sparse Core Ops, SparseCore 0:
  15.7 45.1 all-gather.11
  63.0 48.9 all-gather.9
  121.2 43.4 all-gather.7
  206.3 83.1 reduce-scatter.1
